TPU v7x, 256 devices: a whole 4x4x8 slice. The times are simulated.
256 devices in a mesh: dp: 4 (over x), ctx: 64 (over z, y, core).
Axes of the slice: x: 4, y: 4, z: 8, core: 2. Of those that a mesh axis runs over, the one named last changes fastest.
Arguments:
- queries: bfloat16 [2, 32768, 2048], P(None, ('dp', 'ctx')), may hold values from -6 to 6
- keys: bfloat16 [2, 32768, 1024], P(None, ('dp', 'ctx')), may hold values from -6 to 6
- values: bfloat16 [2, 32768, 1024], P(None, ('dp', 'ctx')), may hold values from -6 to 6
- doc_start: int32 [2, 32768], P(None, ('dp', 'ctx')), may hold values from 0 to 16383, as said below
- gain_q: float32 [128], replicated, may hold values from 0.5 to 1.5
- key_norm_gain: float32 [128], replicated, may hold values from 0.5 to 1.5
- cotangent: bfloat16 [2, 32768, 2048], P(None, ('dp', 'ctx')), may hold values from -6 to 6
Outputs:
- attended: bfloat16 [2, 32768, 2048], P(None, ('dp', 'ctx'))
- grad_queries: bfloat16 [2, 32768, 2048], P(None, ('dp', 'ctx'))
- grad_keys: bfloat16 [2, 32768, 1024], P(None, ('dp', 'ctx'))
- value_gradients: bfloat16 [2, 32768, 1024], P(None, ('dp', 'ctx'))
- grad_gain_q: float32 [128], replicated
- grad_gain_k: float32 [128], replicated
Inputs may be any that keep to these rules, and one draw needn't show every extreme that they name: doc_start gives each token the position in its sequence of its document's first token; the documents of a sequence are runs of 1 to 256 tokens, the first starting at 0, and every sequence has one of exactly 256 tokens.
All inputs are finite; a program needn't handle non-finite values.
Results may differ from a plain program's by a relative error of at most 0.012.
Values may be sent and summed in bfloat16 or wider, within the bound.
No kernel may reach another device: no remote copies, remote signals or barrier semaphores. Data moves between devices by JAX's collectives and lax.ppermute only.
A program may use at most 128 MiB of HBM per device.

v0:
```python
from functools import partial
import jax
import jax.numpy as jnp
from jax import lax
from jax.sharding import PartitionSpec as P

REACH = 2
query_factor = 168.0 ** (-0.5)
rotary_base = 1000000.0
norm_epsilon = 1e-06


def from_behind(block, axis, distance):
    devices = range(lax.axis_size(axis))
    route = [(i - distance, i) for i in devices if i - distance in devices]
    return lax.ppermute(block, axis, route)


def rotary_angles(position, head_width):
    exponent = jnp.arange(head_width // 2, dtype=jnp.float32) * (2.0 / head_width)
    frequency = jnp.exp(-exponent * jnp.log(jnp.float32(rotary_base)))
    return position.astype(jnp.float32)[..., None] * frequency


def prepare(tensor, gain, angle, factor):
    inverse = lax.rsqrt(jnp.mean(tensor * tensor, axis=-1, keepdims=True) + norm_epsilon)
    normed = tensor * inverse * gain
    middle = tensor.shape[-1] // 2
    cosine = jnp.cos(angle)[..., None, :]
    sine = jnp.sin(angle)[..., None, :]
    first = normed[..., :middle]
    second = normed[..., middle:]
    return (
        jnp.concatenate([first * cosine - second * sine, second * cosine + first * sine], axis=-1)
        * factor
    )


def slot_positions(slot, rows, group, block):
    ascending = slot * block + rows
    descending = slot * block + block - 1 - rows
    inside = (slot >= 0) & (slot < 2 * group)
    return jnp.where(inside, jnp.where(slot < group, ascending, descending), -1)


def visible(doc_query, query_position, key_position):
    return (doc_query[:, :, None] <= key_position[:, None, :]) & (
        key_position[:, None, :] <= query_position[:, :, None]
    )


def forward_terms(q_rot, key_panel, value_panel, mask):
    scores = jnp.einsum("xihrd,xjhd->xhrij", q_rot, key_panel, preferred_element_type=jnp.float32)
    weights = jnp.where(mask[:, None, None], jnp.exp(scores), 0.0)
    summed = jnp.sum(weights, axis=-1)
    mixed = jnp.einsum(
        "xhrij,xjhd->xihrd",
        weights.astype(jnp.bfloat16),
        value_panel,
        preferred_element_type=jnp.float32,
    )
    return (summed, mixed)


def softmax_grads(q_rot, cotangent_heads, key_panel, value_panel, mask, total, delta):
    scores = jnp.einsum("xihrd,xjhd->xhrij", q_rot, key_panel, preferred_element_type=jnp.float32)
    probs = jnp.where(mask[:, None, None], jnp.exp(scores) / total[..., None], 0.0)
    dprob = jnp.einsum(
        "xihrd,xjhd->xhrij", cotangent_heads, value_panel, preferred_element_type=jnp.float32
    )
    dscore = probs * (dprob - delta[..., None])
    return (probs.astype(jnp.bfloat16), dscore.astype(jnp.bfloat16))


def key_grads(probs, dscore, q_rot, cotangent_heads):
    grad_key = jnp.einsum("xhrij,xihrd->xjhd", dscore, q_rot, preferred_element_type=jnp.float32)
    grad_value = jnp.einsum(
        "xhrij,xihrd->xjhd", probs, cotangent_heads, preferred_element_type=jnp.float32
    )
    return (grad_key, grad_value)


def all_grads(q_rot, cotangent_heads, key_panel, value_panel, mask, total, delta):
    probs, dscore = softmax_grads(
        q_rot, cotangent_heads, key_panel, value_panel, mask, total, delta
    )
    grad_key, grad_value = key_grads(probs, dscore, q_rot, cotangent_heads)
    grad_query = jnp.einsum(
        "xhrij,xjhd->xihrd", dscore, key_panel, preferred_element_type=jnp.float32
    )
    return (grad_query, grad_key, grad_value)


def advance(lower, upper, at_fold):
    moved_lower = from_behind(lower, "ctx", 1)
    moved_upper = from_behind(upper, "ctx", -1)
    return (moved_lower, jnp.where(at_fold, lower, moved_upper))


def retreat_grads(lower, upper, at_fold, at_start):
    moved_lower = from_behind(lower, "ctx", -1)
    moved_upper = from_behind(upper, "ctx", 1)
    return (jnp.where(at_fold, upper, moved_lower), jnp.where(at_start, 0.0, moved_upper))


def shards(queries, keys, values, doc_start, gain_q, key_norm_gain, cotangent):
    group = lax.axis_size("ctx")
    block = queries.shape[1]
    head_width = gain_q.shape[0]
    q_heads = queries.shape[2] // head_width
    kv_heads = keys.shape[2] // head_width
    repeat = q_heads // kv_heads
    group_index = lax.axis_index("ctx")
    at_fold = group_index == group - 1
    at_start = group_index == 0
    rows = jnp.arange(block, dtype=jnp.int32)[None, :]
    own_slot = jnp.stack([group_index, 2 * group - 1 - group_index])[:, None]
    own_position = slot_positions(own_slot, rows, group, block)
    angle = rotary_angles(own_position, head_width)
    q_rotated, q_back = jax.vjp(
        lambda tensor, gain: prepare(tensor, gain, angle, query_factor),
        queries.astype(jnp.float32).reshape(2, block, q_heads, head_width),
        gain_q,
    )
    q_rot = q_rotated.astype(jnp.bfloat16).reshape(2, block, kv_heads, repeat, head_width)
    k_rotated, k_back = jax.vjp(
        lambda tensor, gain: prepare(tensor, gain, angle, 1.0),
        keys.astype(jnp.float32).reshape(2, block, kv_heads, head_width),
        key_norm_gain,
    )
    k_rot = k_rotated.astype(jnp.bfloat16)
    cotangent_heads = cotangent.reshape(2, block, kv_heads, repeat, head_width)
    local_key_panel = jnp.stack([k_rot.reshape(2, block, -1), values], axis=1)
    panels = [local_key_panel]
    lower, upper = (local_key_panel[0], local_key_panel[1])
    for step in range(REACH):
        lower, upper = advance(lower, upper, at_fold)
        panels.append(jnp.stack([lower, upper]))
    masks = [
        visible(doc_start, own_position, slot_positions(own_slot - step, rows, group, block))
        for step in range(REACH + 1)
    ]
    zeros_q = jnp.zeros((2, block, kv_heads, repeat, head_width), jnp.float32)
    summed = jnp.zeros((2, kv_heads, repeat, block), jnp.float32)
    mixed = zeros_q
    key_panels = []
    value_panels = []
    for step in range(REACH + 1):
        key_panel = panels[step][:, 0].reshape(2, block, kv_heads, head_width)
        value_panel = panels[step][:, 1].reshape(2, block, kv_heads, head_width)
        key_panels.append(key_panel)
        value_panels.append(value_panel)
        compute = partial(forward_terms, q_rot, key_panel, value_panel, masks[step])
        if step == 0:
            terms = compute()
        else:
            terms = compute()
        summed = summed + terms[0]
        mixed = mixed + terms[1]
    attended_heads = (mixed / jnp.transpose(summed, (0, 3, 1, 2))[..., None]).astype(jnp.bfloat16)
    delta = jnp.einsum(
        "xihrd,xihrd->xhri", cotangent_heads, attended_heads, preferred_element_type=jnp.float32
    )
    grad_q_heads = zeros_q
    for step in range(REACH, -1, -1):
        compute = partial(
            all_grads,
            q_rot,
            cotangent_heads,
            key_panels[step],
            value_panels[step],
            masks[step],
            summed,
            delta,
        )
        if step == 0:
            terms = compute()
        else:
            terms = compute()
        grad_q_heads = grad_q_heads + terms[0]
        contribution = jnp.stack(
            [terms[1].reshape(2, block, -1), terms[2].reshape(2, block, -1)], axis=1
        )
        if step == REACH:
            carried_lower, carried_upper = (contribution[0], contribution[1])
        else:
            carried_lower, carried_upper = retreat_grads(
                carried_lower, carried_upper, at_fold, at_start
            )
            carried_lower = carried_lower + contribution[0]
            carried_upper = carried_upper + contribution[1]
    key_value_gradient = jnp.stack([carried_lower, carried_upper])
    grad_k_heads = key_value_gradient[:, 0].reshape(2, block, kv_heads, head_width)
    grad_v_flat = key_value_gradient[:, 1]
    grad_queries, grad_gain_q = q_back(grad_q_heads.reshape(2, block, q_heads, head_width))
    grad_keys, grad_gain_k = k_back(grad_k_heads)
    grad_gain_q, grad_gain_k = lax.psum((grad_gain_q, grad_gain_k), ("dp", "ctx"))
    return (
        attended_heads.reshape(2, block, -1),
        grad_queries.reshape(2, block, -1).astype(jnp.bfloat16),
        grad_keys.reshape(2, block, -1).astype(jnp.bfloat16),
        grad_v_flat.astype(jnp.bfloat16),
        grad_gain_q,
        grad_gain_k,
    )


def solution(mesh):
    placed = (
        P(None, ("dp", "ctx"), None),
        P(None, ("dp", "ctx"), None),
        P(None, ("dp", "ctx"), None),
        P(None, ("dp", "ctx")),
        P(),
        P(),
        P(None, ("dp", "ctx"), None),
    )
    return jax.shard_map(
        shards,
        mesh=mesh,
        in_specs=placed,
        out_specs=(
            P(None, ("dp", "ctx"), None),
            P(None, ("dp", "ctx"), None),
            P(None, ("dp", "ctx"), None),
            P(None, ("dp", "ctx"), None),
            P(),
            P(),
        ),
        check_vma=False,
    )
```

profile of v0, /device:TPU:1, one launch (start us, length us, event | category | flops | bytes accessed | tf_op | source)
XLA Modules:
  0.0 234.9 jit_solution(2773730723189249938)
XLA Ops:
  8.4 5.1 %collective-permute-start.1 = (bf16[2,128,1024]{1,2,0:T(8,128)(2,1)}, bf16[2,128,1024]{1,2,0:T(8,128)(2,1)}, u32[]{:S(2)}, u32[]{:S(2)}) collective-permute-start(bf16[2,128,1024]{1,2,0:T(8,128)(2,1)} %fusion.65), channel_id=1, source_target_pairs={{1,0},{2,1},{3,2},{4,3},{5,4},{6,5},{7,6},{8,7},{9,8},{10,9},{11,1... | collective-permute-start | bytes 1572872 | tf_op jit(solution)/shard_map/ppermute | solution.py:16
  17.4 2.0 copy.219
  19.3 1.9 copy.220
  21.5 2.9 %fusion.3 = bf16[2,128,8,2,128]{4,1,3,2,0:T(8,128)(2,1)S(1)} fusion(f32[2,128,8,2,64]{4,1,3,2,0:T(8,128)} %bitcast.308, f32[2,128,8,2,64]{4,1,3,2,0:T(8,128)} %bitcast.307), kind=kLoop, calls=%fused_computation.9 | loop fusion | flops 1572864 | bytes 3145728 | tf_op jit(solution)/shard_map/convert_element_type | solution.py:125
  25.4 2.1 broadcast_select_fusion
  27.5 1.9 collective-permute-start
  29.4 2.4 %fusion.15 = (f32[2,8,2,128]{3,2,1,0:T(2,128)}, f32[2,8,128,128,2]{3,2,4,1,0:T(8,128)}) fusion(pred[2,128,128]{1,2,0:T(8,128)(4,1)S(1)} %get-tuple-element.68, bf16[2,128,8,2,128]{4,1,3,2,0:T(8,128)(2,1)S(1)} %fusion.3, bf16[2,128,8,128]{3,1,2,0:T(8,128)(2,1)S(1)} %copy-done.9), kind=kOutput, calls=%fused_computation.48 | convolution fusion | flops 135262208 | bytes 3719168 | tf_op jit(solution)/shard_map/xihrd,xjhd->xhrij/dot_general | solution.py:53
  31.8 3.2 %collective-permute-start.3 = (bf16[2,128,1024]{1,2,0:T(8,128)(2,1)}, bf16[2,128,1024]{1,2,0:T(8,128)(2,1)}, u32[]{:S(2)}, u32[]{:S(2)}) collective-permute-start(bf16[2,128,1024]{1,2,0:T(8,128)(2,1)} %get-tuple-element.48), channel_id=1, source_target_pairs={{1,0},{2,1},{3,2},{4,3},{5,4},{6,5},{7,6},{8,7},{9,8},{10,9},{11,1... | collective-permute-start | bytes 1572872 | tf_op jit(solution)/shard_map/ppermute | solution.py:16
  35.9 2.6 %reshape.655 = bf16[2,128,8,2,128]{4,3,2,1,0:T(2,128)(2,1)} reshape(bf16[2,128,2048]{2,1,0:T(8,128)(2,1)} %param.13) | data formatting | bytes 2097152 | tf_op jit(solution)/shard_map/reshape | solution.py:132
  38.4 3.7 %copy.247 = bf16[2,128,8,2,128]{1,4,3,2,0:T(8,128)(2,1)} copy(bf16[2,128,8,2,128]{4,3,2,1,0:T(2,128)(2,1)} %reshape.655) | data formatting | bytes 2097152 | tf_op jit(solution)/shard_map/reshape | solution.py:132
  42.1 2.7 %collective-permute-start.2 = (bf16[2,128,1024]{1,2,0:T(8,128)(2,1)}, bf16[2,128,1024]{1,2,0:T(8,128)(2,1)S(1)}, u32[]{:S(2)}, u32[]{:S(2)}) collective-permute-start(bf16[2,128,1024]{1,2,0:T(8,128)(2,1)} %collective-permute-done), channel_id=1, source_target_pairs={{0,1},{1,2},{2,3},{3,4},{4,5},{5,6},{6,7},{7,8},{8,9},{9,10},{10,1... | collective-permute-start | bytes 1572872 | tf_op jit(solution)/shard_map/ppermute | solution.py:16
  48.7 2.3 collective-permute-done.2
  54.2 2.4 %bitcast_convert_fusion = (f32[2,8,2,128,128]{3,4,2,1,0:T(8,128)}, bf16[2,128,8,2,128]{1,4,3,2,0:T(8,128)(2,1)}) fusion(f32[2,128,8,2]{1,3,2,0:T(2,128)S(1)} %bitcast.339, f32[2,8,128,2,128]{4,2,3,1,0:T(8,128)S(1)} %fusion.23, f32[2,8,128,2,128]{4,2,3,1,0:T(8,128)S(1)} %fusion.25, f32[2,8,128,128,2]{3,2,4,1,0:T(8,128)S(1)} %copy-done.29, ...), kind=kOutput, calls=%fused_computation.87 | convolution fusion | flops 137887744 | bytes 10010624 | tf_op jit(solution)/shard_map/xhrij,xjhd->xihrd/dot_general | solution.py:56
  56.6 4.2 %copy.285 = f32[2,8,2,128,128]{4,2,1,3,0:T(2,128)} copy(f32[2,8,2,128,128]{3,4,2,1,0:T(8,128)} %get-tuple-element.90) | data formatting | bytes 4194304
  60.8 5.1 %multiply_reduce_fusion = f32[2,8,2,128]{2,1,3,0:T(8,128)} fusion(f32[2,8,2,128,128]{4,2,1,3,0:T(2,128)} %copy.285, bf16[2,128,8,2,128]{4,3,2,1,0:T(2,128)(2,1)} %reshape.655), kind=kLoop, calls=%fused_computation.40 | loop fusion | flops 1568768 | bytes 3162112
  65.9 2.2 copy.286
  68.1 2.5 %fusion.49 = f32[2,8,128,128,1]{2,3,4,1,0:T(8,128)S(1)} fusion(bf16[2,128,8,2,128]{1,4,3,2,0:T(8,128)(2,1)} %copy.247, f32[2,8,128,128,2]{3,2,4,1,0:T(8,128)} %copy-done.13, f32[2,8,2,128]{3,2,1,0:T(2,128)} %bitcast.340, pred[2,128,128]{1,2,0:T(8,128)(4,1)} %get-tuple-element.69), kind=kOutput, calls=%fused_computation.97 | convolution fusion | flops 135790592 | bytes 4243456 | tf_op jit(solution)/shard_map/xhrij,xihrd->xjhd/dot_general | solution.py:77
  75.7 2.1 collective-permute-start.5
  80.8 11.8 %collective-permute-done.5 = f32[2,128,1024]{1,2,0:T(8,128)S(1)} collective-permute-done((f32[2,128,1024]{1,2,0:T(8,128)S(1)}, f32[2,128,1024]{1,2,0:T(8,128)S(1)}, u32[]{:S(2)}, u32[]{:S(2)}) %collective-permute-start.5) | collective-permute-done | bytes 1048608 | tf_op jit(solution)/shard_map/ppermute | solution.py:16
  94.1 1.9 collective-permute-start.4
  96.0 3.6 %collective-permute-start.6 = (f32[2,128,1024]{1,2,0:T(8,128)}, f32[2,128,1024]{1,2,0:T(8,128)}, u32[]{:S(2)}, u32[]{:S(2)}) collective-permute-start(f32[2,128,1024]{1,2,0:T(8,128)} %get-tuple-element.44), channel_id=1, source_target_pairs={{1,0},{2,1},{3,2},{4,3},{5,4},{6,5},{7,6},{8,7},{9,8},{10,9},{11,1... | collective-permute-start | bytes 3145736 | tf_op jit(solution)/shard_map/ppermute | solution.py:16
  101.1 3.3 %copy.325 = f32[2,128,16,64]{3,2,1,0:T(8,128)} copy(f32[2,128,16,64]{1,3,2,0:T(8,128)} %get-tuple-element.58) | data formatting | bytes 2097152
  104.4 3.3 %copy.326 = f32[2,128,16,64]{3,2,1,0:T(8,128)} copy(f32[2,128,16,64]{1,3,2,0:T(8,128)} %get-tuple-element.59) | data formatting | bytes 2097152
  107.7 1.9 fusion.89
  112.5 3.0 %fusion.32 = (f32[1,2,128,1024]{2,3,1,0:T(8,128)S(1)}, f32[2,128,1024]{1,2,0:T(8,128)}) fusion(f32[2,1,128,1024]{2,3,1,0:T(8,128)S(1)} %bitcast.301, f32[2,1,128,1024]{2,3,1,0:T(8,128)S(1)} %bitcast.319, f32[2,128,1024]{1,2,0:T(8,128)} %collective-permute-done.6, pred[]{:T(512)S(6)} %eq.6, f32[2,1,128,1024]{2,3,1,0:T(8,128)S(1)} %bitcast.323, ...), kind=kLoop, calls=%fused_computation.63 | loop fusion | flops 1572864 | bytes 8388610 | tf_op jit(solution)/shard_map/stack | solution.py:192
  115.5 2.0 collective-permute-start.7
  118.2 2.5 %multiply_reduce_fusion.1 = (f32[128]{0:T(128)}, f32[2,128,16]{2,1,0:T(8,128)}) fusion(f32[2,128,16]{2,1,0:T(8,128)S(1)} %copy.218, f32[2,128,16,64]{3,2,1,0:T(8,128)S(1)} %get-tuple-element.53, f32[2,128,16,64]{3,2,1,0:T(8,128)S(1)} %get-tuple-element.52, f32[128]{0:T(128)S(1)} %copy-done.60, f32[2,128,16,128]{3,2,1,0:T(8,128)S(1)} %bitcast.299), kind=kLoop, calls=%fused_computation.41 | loop fusion | flops 3665792 | bytes 4228096 | tf_op jit(solution)/shard_map/transpose(jvp())/reduce_sum | solution.py:27
  120.7 1.6 copy.242
  125.1 4.8 %fusion = bf16[2,128,16,128]{3,2,1,0:T(8,128)(2,1)} fusion(f32[2,128,16]{2,1,0:T(8,128)} %copy.243, f32[128]{0:T(128)} %param.11, f32[2,128,16]{2,1,0:T(8,128)S(1)} %copy.218, f32[2,128,16,64]{3,2,1,0:T(8,128)} %copy-done.1, f32[2,128,16,64]{3,2,1,0:T(8,128)} %copy-done, f32[2,128,16,128]{3,2,1,0:T(8,128)S(1)} %bitcast.300), kind=kLoop, calls=%fused_computation.1 | loop fusion | flops 3670016 | bytes 5276160 | tf_op jit(solution)/shard_map/convert_element_type | solution.py:200
  129.9 2.4 %convert_element_type.84 = bf16[2,128,2048]{2,1,0:T(8,128)(2,1)} reshape(bf16[2,128,16,128]{3,2,1,0:T(8,128)(2,1)} %fusion) | data formatting | bytes 2097152 | tf_op jit(solution)/shard_map/convert_element_type | solution.py:200
  139.0 1.6 multiply_add_fusion.4
  143.9 91.0 %all-reduce.4 = (f32[128]{0:T(128)}, f32[128]{0:T(128)}) all-reduce(f32[128]{0:T(128)S(1)} %copy-done.72, f32[128]{0:T(128)S(1)} %get-tuple-element.38), channel_id=1, replica_groups=mesh['dp'=4,'ctx'=64] {'dp','ctx'}, use_global_device_ids=true, to_apply=%region_8.9 | all-reduce | flops 256 | bytes 2048 | tf_op jit(solution)/shard_map/psum | solution.py:197
  (216 shorter events, 47.2 us)
Async XLA Ops:
  0.6 4.8 %copy-start.61 = (f32[128]{0:T(128)S(1)}, f32[128]{0:T(128)}, u32[]{:S(2)}) copy-start(f32[128]{0:T(128)} %param.12) | copy-start | bytes 1540
  6.5 7.1 %copy-start.8 = (bf16[2,128,8,128]{3,1,2,0:T(8,128)(2,1)}, bf16[2,128,8,128]{3,1,2,0:T(8,128)(2,1)S(1)}, u32[]{:S(2)}) copy-start(bf16[2,128,8,128]{3,1,2,0:T(8,128)(2,1)S(1)} %maximum_convert_fusion) | copy-start | bytes 1572868
  7.2 6.3 %copy-start.19 = (bf16[2,128,8,128]{1,3,2,0:T(8,128)(2,1)}, bf16[2,128,8,128]{1,3,2,0:T(8,128)(2,1)S(1)}, u32[]{:S(2)}) copy-start(bf16[2,128,8,128]{1,3,2,0:T(8,128)(2,1)S(1)} %copy.223) | copy-start | bytes 1572868
  7.5 6.1 %copy-start.21 = (bf16[2,128,1024]{1,2,0:T(8,128)(2,1)}, bf16[2,128,1024]{1,2,0:T(8,128)(2,1)S(1)}, u32[]{:S(2)}) copy-start(bf16[2,128,1024]{1,2,0:T(8,128)(2,1)S(1)} %copy.224) | copy-start | bytes 1572868
  8.4 17.0 %collective-permute-start.1 = (bf16[2,128,1024]{1,2,0:T(8,128)(2,1)}, bf16[2,128,1024]{1,2,0:T(8,128)(2,1)}, u32[]{:S(2)}, u32[]{:S(2)}) collective-permute-start(bf16[2,128,1024]{1,2,0:T(8,128)(2,1)} %fusion.65), channel_id=1, source_target_pairs={{1,0},{2,1},{3,2},{4,3},{5,4},{6,5},{7,6},{8,7},{9,8},{10,9},{11,1... | collective-permute-start | bytes 1572872 | tf_op jit(solution)/shard_map/ppermute | solution.py:16
  21.4 3.1 %copy-start.63 = (pred[2]{0:T(512)(128)(4,1)S(1)}, pred[2]{0:T(512)(128)(4,1)}, u32[]{:S(2)}) copy-start(pred[2]{0:T(512)(128)(4,1)} %get-tuple-element.78) | copy-start | bytes 10
  21.4 3.1 %copy-start.64 = (pred[2]{0:T(512)(128)(4,1)S(1)}, pred[2]{0:T(512)(128)(4,1)}, u32[]{:S(2)}) copy-start(pred[2]{0:T(512)(128)(4,1)} %get-tuple-element.79) | copy-start | bytes 10
  21.4 3.1 %copy-start.65 = (pred[2]{0:T(512)(128)(4,1)S(1)}, pred[2]{0:T(512)(128)(4,1)}, u32[]{:S(2)}) copy-start(pred[2]{0:T(512)(128)(4,1)} %get-tuple-element.80) | copy-start | bytes 10
  21.4 3.1 %copy-start.66 = (pred[2]{0:T(512)(128)(4,1)S(1)}, pred[2]{0:T(512)(128)(4,1)}, u32[]{:S(2)}) copy-start(pred[2]{0:T(512)(128)(4,1)} %get-tuple-element.81) | copy-start | bytes 10
  21.4 3.1 %copy-start.67 = (s32[2]{0:T(128)S(1)}, s32[2]{0:T(128)}, u32[]{:S(2)}) copy-start(s32[2]{0:T(128)} %get-tuple-element.46) | copy-start | bytes 28
  21.5 3.1 %copy-start.58 = (s32[2,128]{1,0:T(2,128)S(1)}, s32[2,128]{1,0:T(2,128)}, u32[]{:S(2)}) copy-start(s32[2,128]{1,0:T(2,128)} %get-tuple-element.51) | copy-start | bytes 3076
  21.5 3.1 %copy-start.71 = (s32[2,128]{1,0:T(2,128)S(1)}, s32[2,128]{1,0:T(2,128)}, u32[]{:S(2)}) copy-start(s32[2,128]{1,0:T(2,128)} %param.10) | copy-start | bytes 3076
  21.5 3.9 %copy-start.20 = (bf16[2,128,8,128]{1,3,2,0:T(8,128)(2,1)S(1)}, bf16[2,128,8,128]{1,3,2,0:T(8,128)(2,1)}, u32[]{:S(2)}) copy-start(bf16[2,128,8,128]{1,3,2,0:T(8,128)(2,1)} %copy-done.19) | copy-start | bytes 1572868
  21.5 3.9 %copy-start.22 = (bf16[2,128,1024]{1,2,0:T(8,128)(2,1)S(1)}, bf16[2,128,1024]{1,2,0:T(8,128)(2,1)}, u32[]{:S(2)}) copy-start(bf16[2,128,1024]{1,2,0:T(8,128)(2,1)} %copy-done.21) | copy-start | bytes 1572868
  24.4 5.0 %copy-start.9 = (bf16[2,128,8,128]{3,1,2,0:T(8,128)(2,1)S(1)}, bf16[2,128,8,128]{3,1,2,0:T(8,128)(2,1)}, u32[]{:S(2)}) copy-start(bf16[2,128,8,128]{3,1,2,0:T(8,128)(2,1)} %copy-done.8) | copy-start | bytes 1572868
  25.4 6.4 %copy-start.49 = (pred[2,128,128]{1,2,0:T(8,128)(4,1)}, pred[2,128,128]{1,2,0:T(8,128)(4,1)S(1)}, u32[]{:S(2)}) copy-start(pred[2,128,128]{1,2,0:T(8,128)(4,1)S(1)} %get-tuple-element.68) | copy-start | bytes 98308
  27.5 14.6 %collective-permute-start = (bf16[2,128,1024]{1,2,0:T(8,128)(2,1)}, bf16[2,128,1024]{1,2,0:T(8,128)(2,1)}, u32[]{:S(2)}, u32[]{:S(2)}) collective-permute-start(bf16[2,128,1024]{1,2,0:T(8,128)(2,1)} %get-tuple-element.49), channel_id=1, source_target_pairs={{0,1},{1,2},{2,3},{3,4},{4,5},{5,6},{6,7},{7,8},{8,9},{9,10},{10,1... | collective-permute-start | bytes 1572872 | tf_op jit(solution)/shard_map/ppermute | solution.py:16
  31.8 14.9 %collective-permute-start.3 = (bf16[2,128,1024]{1,2,0:T(8,128)(2,1)}, bf16[2,128,1024]{1,2,0:T(8,128)(2,1)}, u32[]{:S(2)}, u32[]{:S(2)}) collective-permute-start(bf16[2,128,1024]{1,2,0:T(8,128)(2,1)} %get-tuple-element.48), channel_id=1, source_target_pairs={{1,0},{2,1},{3,2},{4,3},{5,4},{6,5},{7,6},{8,7},{9,8},{10,9},{11,1... | collective-permute-start | bytes 1572872 | tf_op jit(solution)/shard_map/ppermute | solution.py:16
  42.1 4.0 %copy-start.43 = (pred[2,128,128]{1,2,0:T(8,128)(4,1)S(1)}, pred[2,128,128]{1,2,0:T(8,128)(4,1)}, u32[]{:S(2)}) copy-start(pred[2,128,128]{1,2,0:T(8,128)(4,1)} %get-tuple-element.70) | copy-start | bytes 98308
  42.1 8.9 %collective-permute-start.2 = (bf16[2,128,1024]{1,2,0:T(8,128)(2,1)}, bf16[2,128,1024]{1,2,0:T(8,128)(2,1)S(1)}, u32[]{:S(2)}, u32[]{:S(2)}) collective-permute-start(bf16[2,128,1024]{1,2,0:T(8,128)(2,1)} %collective-permute-done), channel_id=1, source_target_pairs={{0,1},{1,2},{2,3},{3,4},{4,5},{5,6},{6,7},{7,8},{8,9},{9,10},{10,1... | collective-permute-start | bytes 1572872 | tf_op jit(solution)/shard_map/ppermute | solution.py:16
  53.1 3.5 %copy-start.56 = (f32[2,2,8,128]{3,2,1,0:T(8,128)}, f32[2,2,8,128]{3,2,1,0:T(8,128)S(1)}, u32[]{:S(2)}) copy-start(f32[2,2,8,128]{3,2,1,0:T(8,128)S(1)} %add_add_fusion.2) | copy-start | bytes 49156
  75.1 3.1 %copy-start.26 = (bf16[2,8,2,128,128]{3,4,2,1,0:T(8,128)(2,1)}, bf16[2,8,2,128,128]{3,4,2,1,0:T(8,128)(2,1)S(1)}, u32[]{:S(2)}) copy-start(bf16[2,8,2,128,128]{3,4,2,1,0:T(8,128)(2,1)S(1)} %fusion.5) | copy-start | bytes 3145732
  75.7 16.9 %collective-permute-start.5 = (f32[2,128,1024]{1,2,0:T(8,128)S(1)}, f32[2,128,1024]{1,2,0:T(8,128)S(1)}, u32[]{:S(2)}, u32[]{:S(2)}) collective-permute-start(f32[2,128,1024]{1,2,0:T(8,128)S(1)} %fusion.44), channel_id=1, source_target_pairs={{1,0},{2,1},{3,2},{4,3},{5,4},{6,5},{7,6},{8,7},{9,8},{10,9},{11,1... | collective-permute-start | bytes 3145736 | tf_op jit(solution)/shard_map/ppermute | solution.py:16
  79.8 12.9 %copy-start.6 = (f32[2,8,128,128,1]{3,2,4,1,0:T(8,128)}, f32[2,8,128,128,1]{3,2,4,1,0:T(8,128)S(1)}, u32[]{:S(2)}) copy-start(f32[2,8,128,128,1]{3,2,4,1,0:T(8,128)S(1)} %fusion.88) | copy-start | bytes 3145732
  80.8 13.3 %copy-start.27 = (f32[2,8,128,128,1]{2,3,4,1,0:T(8,128)}, f32[2,8,128,128,1]{2,3,4,1,0:T(8,128)S(1)}, u32[]{:S(2)}) copy-start(f32[2,8,128,128,1]{2,3,4,1,0:T(8,128)S(1)} %fusion.47) | copy-start | bytes 3145732
  94.1 17.3 %collective-permute-start.4 = (f32[2,128,1024]{1,2,0:T(8,128)}, f32[2,128,1024]{1,2,0:T(8,128)}, u32[]{:S(2)}, u32[]{:S(2)}) collective-permute-start(f32[2,128,1024]{1,2,0:T(8,128)} %get-tuple-element.45), channel_id=1, source_target_pairs={{0,1},{1,2},{2,3},{3,4},{4,5},{5,6},{6,7},{7,8},{8,9},{9,10},{10,1... | collective-permute-start | bytes 3145736 | tf_op jit(solution)/shard_map/ppermute | solution.py:16
  96.0 16.4 %collective-permute-start.6 = (f32[2,128,1024]{1,2,0:T(8,128)}, f32[2,128,1024]{1,2,0:T(8,128)}, u32[]{:S(2)}, u32[]{:S(2)}) collective-permute-start(f32[2,128,1024]{1,2,0:T(8,128)} %get-tuple-element.44), channel_id=1, source_target_pairs={{1,0},{2,1},{3,2},{4,3},{5,4},{6,5},{7,6},{8,7},{9,8},{10,9},{11,1... | collective-permute-start | bytes 3145736 | tf_op jit(solution)/shard_map/ppermute | solution.py:16
  111.3 4.2 %copy-start.25 = (f32[2,8,128,128,1]{2,3,4,1,0:T(8,128)}, f32[2,8,128,128,1]{2,3,4,1,0:T(8,128)S(1)}, u32[]{:S(2)}) copy-start(f32[2,8,128,128,1]{2,3,4,1,0:T(8,128)S(1)} %fusion.45) | copy-start | bytes 3145732
  112.4 5.1 %copy-start.15 = (f32[2,128,16,64]{3,2,1,0:T(8,128)S(1)}, f32[2,128,16,64]{3,2,1,0:T(8,128)}, u32[]{:S(2)}) copy-start(f32[2,128,16,64]{3,2,1,0:T(8,128)} %copy.325) | copy-start | bytes 3145732
  112.5 5.1 %copy-start.16 = (f32[2,128,16,64]{3,2,1,0:T(8,128)S(1)}, f32[2,128,16,64]{3,2,1,0:T(8,128)}, u32[]{:S(2)}) copy-start(f32[2,128,16,64]{3,2,1,0:T(8,128)} %copy.326) | copy-start | bytes 3145732
  115.5 18.2 %collective-permute-start.7 = (f32[2,128,1024]{1,2,0:T(8,128)}, f32[2,128,1024]{1,2,0:T(8,128)}, u32[]{:S(2)}, u32[]{:S(2)}) collective-permute-start(f32[2,128,1024]{1,2,0:T(8,128)} %get-tuple-element.43), channel_id=1, source_target_pairs={{0,1},{1,2},{2,3},{3,4},{4,5},{5,6},{6,7},{7,8},{8,9},{9,10},{10,1... | collective-permute-start | bytes 3145736 | tf_op jit(solution)/shard_map/ppermute | solution.py:16
  129.9 3.8 %copy-start.5 = (f32[2,8,128,128,1]{3,2,4,1,0:T(8,128)S(1)}, f32[2,8,128,128,1]{3,2,4,1,0:T(8,128)}, u32[]{:S(2)}) copy-start(f32[2,8,128,128,1]{3,2,4,1,0:T(8,128)} %copy-done.4) | copy-start | bytes 3145732
  (49 other events, 103.0 us)
where the time goes:
time: 236 us; the launch traced here: 235 us
  blocking collectives  91 us (39%)
  local copies, waits for them, and re-layouts  45.8 us (19%)
  other arithmetic  40.8 us (17%)
  starting transfers between devices  22.5 us (10%)
  matrix products  17.9 us (8%)
  waiting for transfers between devices  15.2 us (6%)
    psum x1, blocking collectives, shards(): lax.psum((grad_gain_q, grad_gain_k), ('dp', 'ctx'))  91 us
    unnamed x158, local copies, waits for them, and re-layouts  24.7 us
    ppermute x8, starting transfers between devices, from_behind(): return lax.ppermute(block, axis, route)  22.5 us
    ppermute x8, waiting for transfers between devices, from_behind(): return lax.ppermute(block, axis, route)  15.2 us
    reshape x2, local copies, waits for them, and re-layouts, shards(): cotangent_heads = cotangent.reshape(2, block, kv_heads, repeat, head_width)  6.23 us
    unnamed x1, other arithmetic  5.11 us
    convert_element_type x1, other arithmetic, shards(): grad_queries.reshape(2, block, -1).astype(jnp.bfloat16)  4.83 us
  transfers between devices with their start and end apart: 8, of which 3 were waited for; matrix products, arithmetic and copies ran while one was open for 23% of the time, Pallas kernels for 0%

commit v1 on v0

--- a/solution.py
+++ b/solution.py
@@ -194,7 +194,7 @@
     grad_v_flat = key_value_gradient[:, 1]
     grad_queries, grad_gain_q = q_back(grad_q_heads.reshape(2, block, q_heads, head_width))
     grad_keys, grad_gain_k = k_back(grad_k_heads)
-    grad_gain_q, grad_gain_k = lax.psum((grad_gain_q, grad_gain_k), ("dp", "ctx"))
+    grad_gain_q, grad_gain_k = lax.psum(lax.psum((grad_gain_q, grad_gain_k), "dp"), "ctx")
     return (
         attended_heads.reshape(2, block, -1),
         grad_queries.reshape(2, block, -1).astype(jnp.bfloat16),

time: 236 us -> 292 us (1.24)
  the two profiles are of different devices: /device:TPU:1 before, /device:TPU:128 now
where the time goes in v1:
time: 292 us; the launch traced here: 291 us
  blocking collectives  136 us (47%)
  local copies, waits for them, and re-layouts  45.8 us (16%)
  other arithmetic  40.7 us (14%)
  starting transfers between devices  28.3 us (10%)
  waiting for transfers between devices  19.8 us (7%)
  matrix products  17.9 us (6%)
    psum x1, blocking collectives, shards(): lax.psum(lax.psum((grad_gain_q, grad_gain_k), 'dp'), 'ctx')  126 us
    ppermute x8, starting transfers between devices, from_behind(): return lax.ppermute(block, axis, route)  28.3 us
    unnamed x158, local copies, waits for them, and re-layouts  24.7 us
    ppermute x8, waiting for transfers between devices, from_behind(): return lax.ppermute(block, axis, route)  19.8 us
    psum x1, blocking collectives, shards(): lax.psum((grad_gain_q, grad_gain_k), 'dp')  10.5 us
    reshape x2, local copies, waits for them, and re-layouts, shards(): cotangent_heads = cotangent.reshape(2, block, kv_heads, repeat, head_width)  6.24 us
  transfers between devices with their start and end apart: 8, of which 4 were waited for; matrix products, arithmetic and copies ran while one was open for 19% of the time, Pallas kernels for 0%

profile of v1, /device:TPU:128, one launch (start us, length us, event | category | flops | bytes accessed | tf_op | source)
XLA Modules:
  0.0 290.6 jit_solution(11939150100067765988)
XLA Ops:
  8.4 3.9 %collective-permute-start.1 = (bf16[2,128,1024]{1,2,0:T(8,128)(2,1)}, bf16[2,128,1024]{1,2,0:T(8,128)(2,1)}, u32[]{:S(2)}, u32[]{:S(2)}) collective-permute-start(bf16[2,128,1024]{1,2,0:T(8,128)(2,1)} %fusion.65), channel_id=1, source_target_pairs={{1,0},{2,1},{3,2},{4,3},{5,4},{6,5},{7,6},{8,7},{9,8},{10,9},{11,1... | collective-permute-start | bytes 1572872 | tf_op jit(solution)/shard_map/ppermute | solution.py:16
  16.1 2.0 copy.219
  18.0 2.0 copy.220
  20.2 2.9 %fusion.3 = bf16[2,128,8,2,128]{4,1,3,2,0:T(8,128)(2,1)S(1)} fusion(f32[2,128,8,2,64]{4,1,3,2,0:T(8,128)} %bitcast.308, f32[2,128,8,2,64]{4,1,3,2,0:T(8,128)} %bitcast.307), kind=kLoop, calls=%fused_computation.9 | loop fusion | flops 1572864 | bytes 3145728 | tf_op jit(solution)/shard_map/convert_element_type | solution.py:125
  24.2 2.1 broadcast_select_fusion
  26.2 1.9 collective-permute-start
  28.2 2.4 fusion.15
  30.6 7.0 %collective-permute-start.3 = (bf16[2,128,1024]{1,2,0:T(8,128)(2,1)}, bf16[2,128,1024]{1,2,0:T(8,128)(2,1)}, u32[]{:S(2)}, u32[]{:S(2)}) collective-permute-start(bf16[2,128,1024]{1,2,0:T(8,128)(2,1)} %get-tuple-element.50), channel_id=1, source_target_pairs={{1,0},{2,1},{3,2},{4,3},{5,4},{6,5},{7,6},{8,7},{9,8},{10,9},{11,1... | collective-permute-start | bytes 1572872 | tf_op jit(solution)/shard_map/ppermute | solution.py:16
  38.4 2.6 reshape.655
  40.9 3.7 %copy.247 = bf16[2,128,8,2,128]{1,4,3,2,0:T(8,128)(2,1)} copy(bf16[2,128,8,2,128]{4,3,2,1,0:T(2,128)(2,1)} %reshape.655) | data formatting | bytes 2097152 | tf_op jit(solution)/shard_map/reshape | solution.py:132
  44.6 2.2 collective-permute-start.2
  50.8 8.0 %collective-permute-done.2 = bf16[2,128,1024]{1,2,0:T(8,128)(2,1)S(1)} collective-permute-done((bf16[2,128,1024]{1,2,0:T(8,128)(2,1)}, bf16[2,128,1024]{1,2,0:T(8,128)(2,1)S(1)}, u32[]{:S(2)}, u32[]{:S(2)}) %collective-permute-start.2) | collective-permute-done | bytes 524320 | tf_op jit(solution)/shard_map/ppermute | solution.py:16
  62.0 2.4 bitcast_convert_fusion
  64.3 4.2 %copy.285 = f32[2,8,2,128,128]{4,2,1,3,0:T(2,128)} copy(f32[2,8,2,128,128]{3,4,2,1,0:T(8,128)} %get-tuple-element.92) | data formatting | bytes 4194304
  68.5 5.1 %multiply_reduce_fusion = f32[2,8,2,128]{2,1,3,0:T(8,128)} fusion(f32[2,8,2,128,128]{4,2,1,3,0:T(2,128)} %copy.285, bf16[2,128,8,2,128]{4,3,2,1,0:T(2,128)(2,1)} %reshape.655), kind=kLoop, calls=%fused_computation.40 | loop fusion | flops 1568768 | bytes 3162112
  73.6 2.2 copy.286
  75.8 2.5 fusion.49
  83.5 2.1 collective-permute-start.5
  88.5 9.3 %collective-permute-done.5 = f32[2,128,1024]{1,2,0:T(8,128)S(1)} collective-permute-done((f32[2,128,1024]{1,2,0:T(8,128)S(1)}, f32[2,128,1024]{1,2,0:T(8,128)S(1)}, u32[]{:S(2)}, u32[]{:S(2)}) %collective-permute-start.5) | collective-permute-done | bytes 1048608 | tf_op jit(solution)/shard_map/ppermute | solution.py:16
  99.3 1.9 collective-permute-start.4
  101.2 7.4 %collective-permute-start.6 = (f32[2,128,1024]{1,2,0:T(8,128)}, f32[2,128,1024]{1,2,0:T(8,128)}, u32[]{:S(2)}, u32[]{:S(2)}) collective-permute-start(f32[2,128,1024]{1,2,0:T(8,128)} %get-tuple-element.46), channel_id=1, source_target_pairs={{1,0},{2,1},{3,2},{4,3},{5,4},{6,5},{7,6},{8,7},{9,8},{10,9},{11,1... | collective-permute-start | bytes 3145736 | tf_op jit(solution)/shard_map/ppermute | solution.py:16
  110.1 3.3 %copy.325 = f32[2,128,16,64]{3,2,1,0:T(8,128)} copy(f32[2,128,16,64]{1,3,2,0:T(8,128)} %get-tuple-element.60) | data formatting | bytes 2097152
  113.4 3.3 %copy.326 = f32[2,128,16,64]{3,2,1,0:T(8,128)} copy(f32[2,128,16,64]{1,3,2,0:T(8,128)} %get-tuple-element.61) | data formatting | bytes 2097152
  116.7 1.9 fusion.89
  121.0 3.0 %fusion.32 = (f32[1,2,128,1024]{2,3,1,0:T(8,128)S(1)}, f32[2,128,1024]{1,2,0:T(8,128)}) fusion(f32[2,1,128,1024]{2,3,1,0:T(8,128)S(1)} %bitcast.301, f32[2,1,128,1024]{2,3,1,0:T(8,128)S(1)} %bitcast.319, f32[2,128,1024]{1,2,0:T(8,128)} %collective-permute-done.6, pred[]{:T(512)S(6)} %eq.6, f32[2,1,128,1024]{2,3,1,0:T(8,128)S(1)} %bitcast.323, ...), kind=kLoop, calls=%fused_computation.63 | loop fusion | flops 1572864 | bytes 8388610 | tf_op jit(solution)/shard_map/stack | solution.py:192
  124.0 2.0 collective-permute-start.7
  126.7 2.5 multiply_reduce_fusion.1
  133.6 4.8 %fusion = bf16[2,128,16,128]{3,2,1,0:T(8,128)(2,1)} fusion(f32[2,128,16]{2,1,0:T(8,128)} %copy.243, f32[128]{0:T(128)} %param.11, f32[2,128,16]{2,1,0:T(8,128)S(1)} %copy.218, f32[2,128,16,64]{3,2,1,0:T(8,128)} %copy-done.1, f32[2,128,16,64]{3,2,1,0:T(8,128)} %copy-done, f32[2,128,16,128]{3,2,1,0:T(8,128)S(1)} %bitcast.300), kind=kLoop, calls=%fused_computation.1 | loop fusion | flops 3670016 | bytes 5276160 | tf_op jit(solution)/shard_map/convert_element_type | solution.py:200
  138.5 2.4 convert_element_type.84
  142.2 1.9 collective-permute-done.7
  154.3 10.5 %all-reduce.5 = (f32[128]{0:T(128)S(1)}, f32[128]{0:T(128)S(1)}) all-reduce(f32[128]{0:T(128)S(1)} %copy-done.72, f32[128]{0:T(128)S(1)} %get-tuple-element.38), channel_id=1, replica_groups=mesh['dp'=4,'ctx'=64] {'dp'}, use_global_device_ids=true, to_apply=%region_8.9 | all-reduce | flops 256 | bytes 2048 | tf_op jit(solution)/shard_map/psum | solution.py:197
  164.7 125.9 %all-reduce.4 = (f32[128]{0:T(128)}, f32[128]{0:T(128)}) all-reduce(f32[128]{0:T(128)S(1)} %get-tuple-element.42, f32[128]{0:T(128)S(1)} %get-tuple-element.43), channel_id=1, replica_groups=mesh['dp'=4,'ctx'=64] {'ctx'}, use_global_device_ids=true, to_apply=%region_9.10 | all-reduce | flops 256 | bytes 2048 | tf_op jit(solution)/shard_map/psum | solution.py:197
  (217 shorter events, 49.8 us)
Async XLA Ops:
  0.6 4.7 %copy-start.61 = (f32[128]{0:T(128)S(1)}, f32[128]{0:T(128)}, u32[]{:S(2)}) copy-start(f32[128]{0:T(128)} %param.12) | copy-start | bytes 1540
  6.5 5.8 %copy-start.8 = (bf16[2,128,8,128]{3,1,2,0:T(8,128)(2,1)}, bf16[2,128,8,128]{3,1,2,0:T(8,128)(2,1)S(1)}, u32[]{:S(2)}) copy-start(bf16[2,128,8,128]{3,1,2,0:T(8,128)(2,1)S(1)} %maximum_convert_fusion) | copy-start | bytes 1572868
  7.2 5.1 %copy-start.19 = (bf16[2,128,8,128]{1,3,2,0:T(8,128)(2,1)}, bf16[2,128,8,128]{1,3,2,0:T(8,128)(2,1)S(1)}, u32[]{:S(2)}) copy-start(bf16[2,128,8,128]{1,3,2,0:T(8,128)(2,1)S(1)} %copy.223) | copy-start | bytes 1572868
  7.5 4.8 %copy-start.21 = (bf16[2,128,1024]{1,2,0:T(8,128)(2,1)}, bf16[2,128,1024]{1,2,0:T(8,128)(2,1)S(1)}, u32[]{:S(2)}) copy-start(bf16[2,128,1024]{1,2,0:T(8,128)(2,1)S(1)} %copy.224) | copy-start | bytes 1572868
  8.4 15.8 %collective-permute-start.1 = (bf16[2,128,1024]{1,2,0:T(8,128)(2,1)}, bf16[2,128,1024]{1,2,0:T(8,128)(2,1)}, u32[]{:S(2)}, u32[]{:S(2)}) collective-permute-start(bf16[2,128,1024]{1,2,0:T(8,128)(2,1)} %fusion.65), channel_id=1, source_target_pairs={{1,0},{2,1},{3,2},{4,3},{5,4},{6,5},{7,6},{8,7},{9,8},{10,9},{11,1... | collective-permute-start | bytes 1572872 | tf_op jit(solution)/shard_map/ppermute | solution.py:16
  20.1 3.1 %copy-start.63 = (pred[2]{0:T(512)(128)(4,1)S(1)}, pred[2]{0:T(512)(128)(4,1)}, u32[]{:S(2)}) copy-start(pred[2]{0:T(512)(128)(4,1)} %get-tuple-element.80) | copy-start | bytes 10
  20.1 3.1 %copy-start.64 = (pred[2]{0:T(512)(128)(4,1)S(1)}, pred[2]{0:T(512)(128)(4,1)}, u32[]{:S(2)}) copy-start(pred[2]{0:T(512)(128)(4,1)} %get-tuple-element.81) | copy-start | bytes 10
  20.1 3.1 %copy-start.65 = (pred[2]{0:T(512)(128)(4,1)S(1)}, pred[2]{0:T(512)(128)(4,1)}, u32[]{:S(2)}) copy-start(pred[2]{0:T(512)(128)(4,1)} %get-tuple-element.82) | copy-start | bytes 10
  20.1 3.1 %copy-start.66 = (pred[2]{0:T(512)(128)(4,1)S(1)}, pred[2]{0:T(512)(128)(4,1)}, u32[]{:S(2)}) copy-start(pred[2]{0:T(512)(128)(4,1)} %get-tuple-element.83) | copy-start | bytes 10
  20.2 3.1 %copy-start.58 = (s32[2,128]{1,0:T(2,128)S(1)}, s32[2,128]{1,0:T(2,128)}, u32[]{:S(2)}) copy-start(s32[2,128]{1,0:T(2,128)} %get-tuple-element.53) | copy-start | bytes 3076
  20.2 3.1 %copy-start.71 = (s32[2,128]{1,0:T(2,128)S(1)}, s32[2,128]{1,0:T(2,128)}, u32[]{:S(2)}) copy-start(s32[2,128]{1,0:T(2,128)} %param.10) | copy-start | bytes 3076
  20.2 3.9 %copy-start.20 = (bf16[2,128,8,128]{1,3,2,0:T(8,128)(2,1)S(1)}, bf16[2,128,8,128]{1,3,2,0:T(8,128)(2,1)}, u32[]{:S(2)}) copy-start(bf16[2,128,8,128]{1,3,2,0:T(8,128)(2,1)} %copy-done.19) | copy-start | bytes 1572868
  20.2 3.9 %copy-start.22 = (bf16[2,128,1024]{1,2,0:T(8,128)(2,1)S(1)}, bf16[2,128,1024]{1,2,0:T(8,128)(2,1)}, u32[]{:S(2)}) copy-start(bf16[2,128,1024]{1,2,0:T(8,128)(2,1)} %copy-done.21) | copy-start | bytes 1572868
  23.2 5.0 %copy-start.9 = (bf16[2,128,8,128]{3,1,2,0:T(8,128)(2,1)S(1)}, bf16[2,128,8,128]{3,1,2,0:T(8,128)(2,1)}, u32[]{:S(2)}) copy-start(bf16[2,128,8,128]{3,1,2,0:T(8,128)(2,1)} %copy-done.8) | copy-start | bytes 1572868
  24.1 6.5 %copy-start.49 = (pred[2,128,128]{1,2,0:T(8,128)(4,1)}, pred[2,128,128]{1,2,0:T(8,128)(4,1)S(1)}, u32[]{:S(2)}) copy-start(pred[2,128,128]{1,2,0:T(8,128)(4,1)S(1)} %get-tuple-element.70) | copy-start | bytes 98308
  26.2 18.4 %collective-permute-start = (bf16[2,128,1024]{1,2,0:T(8,128)(2,1)}, bf16[2,128,1024]{1,2,0:T(8,128)(2,1)}, u32[]{:S(2)}, u32[]{:S(2)}) collective-permute-start(bf16[2,128,1024]{1,2,0:T(8,128)(2,1)} %get-tuple-element.51), channel_id=1, source_target_pairs={{0,1},{1,2},{2,3},{3,4},{4,5},{5,6},{6,7},{7,8},{8,9},{9,10},{10,1... | collective-permute-start | bytes 1572872 | tf_op jit(solution)/shard_map/ppermute | solution.py:16
  30.6 18.2 %collective-permute-start.3 = (bf16[2,128,1024]{1,2,0:T(8,128)(2,1)}, bf16[2,128,1024]{1,2,0:T(8,128)(2,1)}, u32[]{:S(2)}, u32[]{:S(2)}) collective-permute-start(bf16[2,128,1024]{1,2,0:T(8,128)(2,1)} %get-tuple-element.50), channel_id=1, source_target_pairs={{1,0},{2,1},{3,2},{4,3},{5,4},{6,5},{7,6},{8,7},{9,8},{10,9},{11,1... | collective-permute-start | bytes 1572872 | tf_op jit(solution)/shard_map/ppermute | solution.py:16
  44.6 3.5 %copy-start.43 = (pred[2,128,128]{1,2,0:T(8,128)(4,1)S(1)}, pred[2,128,128]{1,2,0:T(8,128)(4,1)}, u32[]{:S(2)}) copy-start(pred[2,128,128]{1,2,0:T(8,128)(4,1)} %get-tuple-element.72) | copy-start | bytes 98308
  44.6 14.2 %collective-permute-start.2 = (bf16[2,128,1024]{1,2,0:T(8,128)(2,1)}, bf16[2,128,1024]{1,2,0:T(8,128)(2,1)S(1)}, u32[]{:S(2)}, u32[]{:S(2)}) collective-permute-start(bf16[2,128,1024]{1,2,0:T(8,128)(2,1)} %collective-permute-done), channel_id=1, source_target_pairs={{0,1},{1,2},{2,3},{3,4},{4,5},{5,6},{6,7},{7,8},{8,9},{9,10},{10,1... | collective-permute-start | bytes 1572872 | tf_op jit(solution)/shard_map/ppermute | solution.py:16
  50.8 8.1 %copy-start.45 = (pred[2,128,128]{1,2,0:T(8,128)(4,1)S(1)}, pred[2,128,128]{1,2,0:T(8,128)(4,1)}, u32[]{:S(2)}) copy-start(pred[2,128,128]{1,2,0:T(8,128)(4,1)} %get-tuple-element.71) | copy-start | bytes 98308
  60.9 3.5 %copy-start.56 = (f32[2,2,8,128]{3,2,1,0:T(8,128)}, f32[2,2,8,128]{3,2,1,0:T(8,128)S(1)}, u32[]{:S(2)}) copy-start(f32[2,2,8,128]{3,2,1,0:T(8,128)S(1)} %add_add_fusion.2) | copy-start | bytes 49156
  82.9 3.1 %copy-start.26 = (bf16[2,8,2,128,128]{3,4,2,1,0:T(8,128)(2,1)}, bf16[2,8,2,128,128]{3,4,2,1,0:T(8,128)(2,1)S(1)}, u32[]{:S(2)}) copy-start(bf16[2,8,2,128,128]{3,4,2,1,0:T(8,128)(2,1)S(1)} %fusion.5) | copy-start | bytes 3145732
  83.5 14.4 %collective-permute-start.5 = (f32[2,128,1024]{1,2,0:T(8,128)S(1)}, f32[2,128,1024]{1,2,0:T(8,128)S(1)}, u32[]{:S(2)}, u32[]{:S(2)}) collective-permute-start(f32[2,128,1024]{1,2,0:T(8,128)S(1)} %fusion.44), channel_id=1, source_target_pairs={{1,0},{2,1},{3,2},{4,3},{5,4},{6,5},{7,6},{8,7},{9,8},{10,9},{11,1... | collective-permute-start | bytes 3145736 | tf_op jit(solution)/shard_map/ppermute | solution.py:16
  87.5 10.3 %copy-start.6 = (f32[2,8,128,128,1]{3,2,4,1,0:T(8,128)}, f32[2,8,128,128,1]{3,2,4,1,0:T(8,128)S(1)}, u32[]{:S(2)}) copy-start(f32[2,8,128,128,1]{3,2,4,1,0:T(8,128)S(1)} %fusion.88) | copy-start | bytes 3145732
  88.5 10.8 %copy-start.27 = (f32[2,8,128,128,1]{2,3,4,1,0:T(8,128)}, f32[2,8,128,128,1]{2,3,4,1,0:T(8,128)S(1)}, u32[]{:S(2)}) copy-start(f32[2,8,128,128,1]{2,3,4,1,0:T(8,128)S(1)} %fusion.47) | copy-start | bytes 3145732
  99.3 21.1 %collective-permute-start.4 = (f32[2,128,1024]{1,2,0:T(8,128)}, f32[2,128,1024]{1,2,0:T(8,128)}, u32[]{:S(2)}, u32[]{:S(2)}) collective-permute-start(f32[2,128,1024]{1,2,0:T(8,128)} %get-tuple-element.47), channel_id=1, source_target_pairs={{0,1},{1,2},{2,3},{3,4},{4,5},{5,6},{6,7},{7,8},{8,9},{9,10},{10,1... | collective-permute-start | bytes 3145736 | tf_op jit(solution)/shard_map/ppermute | solution.py:16
  101.2 19.8 %collective-permute-start.6 = (f32[2,128,1024]{1,2,0:T(8,128)}, f32[2,128,1024]{1,2,0:T(8,128)}, u32[]{:S(2)}, u32[]{:S(2)}) collective-permute-start(f32[2,128,1024]{1,2,0:T(8,128)} %get-tuple-element.46), channel_id=1, source_target_pairs={{1,0},{2,1},{3,2},{4,3},{5,4},{6,5},{7,6},{8,7},{9,8},{10,9},{11,1... | collective-permute-start | bytes 3145736 | tf_op jit(solution)/shard_map/ppermute | solution.py:16
  120.3 3.7 %copy-start.25 = (f32[2,8,128,128,1]{2,3,4,1,0:T(8,128)}, f32[2,8,128,128,1]{2,3,4,1,0:T(8,128)S(1)}, u32[]{:S(2)}) copy-start(f32[2,8,128,128,1]{2,3,4,1,0:T(8,128)S(1)} %fusion.45) | copy-start | bytes 3145732
  121.0 5.1 %copy-start.15 = (f32[2,128,16,64]{3,2,1,0:T(8,128)S(1)}, f32[2,128,16,64]{3,2,1,0:T(8,128)}, u32[]{:S(2)}) copy-start(f32[2,128,16,64]{3,2,1,0:T(8,128)} %copy.325) | copy-start | bytes 3145732
  121.0 5.1 %copy-start.16 = (f32[2,128,16,64]{3,2,1,0:T(8,128)S(1)}, f32[2,128,16,64]{3,2,1,0:T(8,128)}, u32[]{:S(2)}) copy-start(f32[2,128,16,64]{3,2,1,0:T(8,128)} %copy.326) | copy-start | bytes 3145732
  124.0 20.1 %collective-permute-start.7 = (f32[2,128,1024]{1,2,0:T(8,128)}, f32[2,128,1024]{1,2,0:T(8,128)}, u32[]{:S(2)}, u32[]{:S(2)}) collective-permute-start(f32[2,128,1024]{1,2,0:T(8,128)} %get-tuple-element.45), channel_id=1, source_target_pairs={{0,1},{1,2},{2,3},{3,4},{4,5},{5,6},{6,7},{7,8},{8,9},{9,10},{10,1... | collective-permute-start | bytes 3145736 | tf_op jit(solution)/shard_map/ppermute | solution.py:16
  138.5 5.6 %copy-start.5 = (f32[2,8,128,128,1]{3,2,4,1,0:T(8,128)S(1)}, f32[2,8,128,128,1]{3,2,4,1,0:T(8,128)}, u32[]{:S(2)}) copy-start(f32[2,8,128,128,1]{3,2,4,1,0:T(8,128)} %copy-done.4) | copy-start | bytes 3145732
  (49 other events, 102.3 us)
